TPU v7x, 256 devices: a whole 4x4x8 slice. The times are simulated.
256 devices in a mesh: dp: 32 (over z_hi, x, core), seq: 8 (over y, z_lo).
Axes of the slice: x: 4, y: 4, z: 8 (z_hi: 4, z_lo: 2; z = z_hi * 2 + z_lo), core: 2. Of those that a mesh axis runs over, the one named last changes fastest.
Arguments:
- q_proj: bfloat16 [32, 1024, 4096], P('dp', 'seq'), may hold values from -200 to 200
- k_proj: bfloat16 [32, 1024, 512], P('dp', 'seq'), may hold values from -6 to 6
- v_proj: bfloat16 [32, 1024, 512], P('dp', 'seq'), may hold values from -6 to 6
- cache_k: bfloat16 [32, 1024, 512], P('dp', 'seq'), may hold values from -6 to 6
- cache_v: bfloat16 [32, 1024, 512], P('dp', 'seq'), may hold values from -6 to 6
- bias_q: bfloat16 [4096], replicated, may hold values from -3 to 3
- bias_k: bfloat16 [512], replicated, may hold values from -3 to 3
- bias_v: bfloat16 [512], replicated, may hold values from -3 to 3
- start: int32 [32], P('dp'), may hold values from 256 to 1024, as said below
- dout: bfloat16 [32, 1024, 4096], P('dp', 'seq'), may hold values from -6 to 6
Outputs:
- attn_out: bfloat16 [32, 1024, 4096], P('dp', 'seq')
- grad_q: bfloat16 [32, 1024, 4096], P('dp', 'seq')
- grad_k: bfloat16 [32, 1024, 512], P('dp', 'seq')
- grad_v: bfloat16 [32, 1024, 512], P('dp', 'seq')
- grad_bias_q: float32 [4096], replicated
- grad_bias_k: float32 [512], replicated
- grad_bias_v: float32 [512], replicated
Inputs may be any that keep to these rules, and one draw needn't show every extreme that they name: Cache slots at and beyond start hold no prefix; some sequence has a full prefix of 1024 slots.
All inputs are finite; a program needn't handle non-finite values.
Results may differ from a plain program's by a relative error of at most 0.04.
The roundings to bfloat16 on the way count: a program that leaves them out, or rounds other values in their place, can miss the bound.
Values may be sent and summed in bfloat16 or wider, within the bound.
A program may use at most 128 MiB of HBM per device.

v0:
```python
import jax
import jax.numpy as jnp
from jax import lax
from jax.sharding import PartitionSpec as P

HQ = 32
KV = 4
HD = 128
GROUP = 8


def rotary_tables(positions, width):
    half = width // 2
    freqs = jnp.exp(
        -(2.0 * jnp.arange(half, dtype=jnp.float32) / width) * jnp.log(jnp.float32(1000000.0))
    )
    angles = positions.astype(jnp.float32)[:, None] * freqs[None, :]
    cosine = jnp.concatenate([jnp.cos(angles), jnp.cos(angles)], axis=1)
    sine = jnp.concatenate([jnp.sin(angles), jnp.sin(angles)], axis=1)
    return (cosine[:, None, :], sine[:, None, :])


def rotary(values, positions):
    cosine, sine = rotary_tables(positions, values.shape[2])
    half = values.shape[2] // 2
    turned = jnp.concatenate([-values[:, :, half:], values[:, :, :half]], axis=2)
    return values * cosine + turned * sine


def rotary_back(grads, positions):
    cosine, sine = rotary_tables(positions, grads.shape[2])
    half = grads.shape[2] // 2
    scaled = grads * sine
    turned = jnp.concatenate([scaled[:, :, half:], -scaled[:, :, :half]], axis=2)
    return grads * cosine + turned


def attend(queries, cotangent, keys, values, first, row_zero, prefix):
    rows, heads, width = queries.shape
    key_count = keys.shape[0]
    slab = key_count - prefix
    head_block = max(1, min(512 // rows, GROUP, heads))
    row_block = min(rows, 512)
    scale = width ** (-0.5)
    key_index = jnp.arange(key_count, dtype=jnp.int32)

    def head_step(carry, head_slot):
        key_acc, value_acc = carry
        head_zero = head_slot * head_block
        owner = head_zero // GROUP
        key_one = lax.dynamic_index_in_dim(keys, owner, 1, keepdims=False)
        value_one = lax.dynamic_index_in_dim(values, owner, 1, keepdims=False)
        query_part = lax.dynamic_slice_in_dim(queries, head_zero, head_block, 1)
        cot_part = lax.dynamic_slice_in_dim(cotangent, head_zero, head_block, 1)

        def row_step(inner, row_slot):
            grad_key, grad_value = inner
            offset = row_slot * row_block
            query_rows = lax.dynamic_slice_in_dim(query_part, offset, row_block, 0)
            cot_rows = lax.dynamic_slice_in_dim(cot_part, offset, row_block, 0)
            query_index = row_zero + offset + jnp.arange(row_block, dtype=jnp.int32)
            allowed = jnp.where(
                key_index[None, :] < prefix,
                key_index[None, :] < first,
                key_index[None, :] - prefix <= query_index[:, None],
            )
            scores = (
                jnp.einsum("rhd,kd->hrk", query_rows, key_one, preferred_element_type=jnp.float32)
                * scale
            )
            scores = jnp.where(allowed[None], scores, -1e30)
            highest = jnp.max(scores, axis=-1, keepdims=True)
            expo = jnp.exp(scores - highest)
            probs = expo / jnp.sum(expo, axis=-1, keepdims=True)
            probs_b = probs.astype(jnp.bfloat16)
            output = jnp.einsum(
                "hrk,kd->rhd", probs_b, value_one, preferred_element_type=jnp.float32
            ).astype(jnp.bfloat16)
            delta = jnp.sum(cot_rows.astype(jnp.float32) * output.astype(jnp.float32), axis=-1).T
            dprobs = jnp.einsum(
                "rhd,kd->hrk", cot_rows, value_one, preferred_element_type=jnp.float32
            )
            dscore = (probs * (dprobs - delta[:, :, None])).astype(jnp.bfloat16)
            grad_query = (
                jnp.einsum("hrk,kd->rhd", dscore, key_one, preferred_element_type=jnp.float32)
                * scale
            ).astype(jnp.bfloat16)
            grad_key = (
                grad_key
                + jnp.einsum(
                    "hrk,rhd->kd",
                    dscore[:, :, prefix:],
                    query_rows,
                    preferred_element_type=jnp.float32,
                )
                * scale
            )
            grad_value = grad_value + jnp.einsum(
                "hrk,rhd->kd", probs_b[:, :, prefix:], cot_rows, preferred_element_type=jnp.float32
            )
            return ((grad_key, grad_value), (output, grad_query))

        empty = jnp.zeros((slab, width), jnp.float32)
        (grad_key, grad_value), (outputs, grads) = lax.scan(
            row_step, (empty, empty), jnp.arange(rows // row_block, dtype=jnp.int32)
        )
        outputs = outputs.reshape(rows, head_block, width)
        grads = grads.reshape(rows, head_block, width)
        old_key = lax.dynamic_index_in_dim(key_acc, owner, 1, keepdims=False)
        old_value = lax.dynamic_index_in_dim(value_acc, owner, 1, keepdims=False)
        key_acc = lax.dynamic_update_index_in_dim(key_acc, old_key + grad_key, owner, 1)
        value_acc = lax.dynamic_update_index_in_dim(value_acc, old_value + grad_value, owner, 1)
        return ((key_acc, value_acc), (outputs, grads))

    zeros_kv = jnp.zeros((slab, keys.shape[1], width), jnp.float32)
    (key_acc, value_acc), (outputs, grads) = lax.scan(
        head_step, (zeros_kv, zeros_kv), jnp.arange(heads // head_block, dtype=jnp.int32)
    )
    outputs = jnp.transpose(outputs, (1, 0, 2, 3)).reshape(rows, heads, width)
    grads = jnp.transpose(grads, (1, 0, 2, 3)).reshape(rows, heads, width)
    return (outputs, grads, key_acc, value_acc)


def body(q_proj, k_proj, v_proj, cache_k, cache_v, bias_q, bias_k, bias_v, start, dout):
    devices = lax.axis_size("seq")
    rank = lax.axis_index("seq")
    tokens = q_proj.shape[1]
    first = start[0]
    positions = first + rank * tokens + jnp.arange(tokens, dtype=jnp.int32)
    queries = rotary(
        (q_proj[0].astype(jnp.float32) + bias_q.astype(jnp.float32)).reshape(tokens, HQ, HD),
        positions,
    ).astype(jnp.bfloat16)
    keys = rotary(
        (k_proj[0].astype(jnp.float32) + bias_k.astype(jnp.float32)).reshape(tokens, KV, HD),
        positions,
    ).astype(jnp.bfloat16)
    values = (
        (v_proj[0].astype(jnp.float32) + bias_v.astype(jnp.float32))
        .astype(jnp.bfloat16)
        .reshape(tokens, KV, HD)
    )
    cotangent = dout[0].reshape(tokens, HQ, HD)
    cached_keys = cache_k[0].reshape(cache_k.shape[1], KV, HD)
    cached_values = cache_v[0].reshape(cache_v.shape[1], KV, HD)
    copies = max(devices // KV, 1)
    keys_wide = jnp.repeat(keys, copies, axis=1)
    values_wide = jnp.repeat(values, copies, axis=1)
    cache_keys_wide = jnp.repeat(cached_keys, copies, axis=1)
    cache_values_wide = jnp.repeat(cached_values, copies, axis=1)
    head_queries, head_keys, head_values, head_cot = (
        lax.all_to_all(queries, "seq", split_axis=1, concat_axis=0, tiled=True),
        lax.all_to_all(keys_wide, "seq", split_axis=1, concat_axis=0, tiled=True),
        lax.all_to_all(values_wide, "seq", split_axis=1, concat_axis=0, tiled=True),
        lax.all_to_all(cotangent, "seq", split_axis=1, concat_axis=0, tiled=True),
    )
    head_cache_keys, head_cache_values = (
        lax.all_to_all(cache_keys_wide, "seq", split_axis=1, concat_axis=0, tiled=True),
        lax.all_to_all(cache_values_wide, "seq", split_axis=1, concat_axis=0, tiled=True),
    )
    prefix = head_cache_keys.shape[0]
    all_keys = jnp.concatenate([head_cache_keys, head_keys], axis=0)
    all_values = jnp.concatenate([head_cache_values, head_values], axis=0)
    outputs, dq_rot, dk_rot, dv_all = attend(
        head_queries, head_cot, all_keys, all_values, first, 0, prefix
    )
    out_tokens, dq_tokens = (
        lax.all_to_all(outputs, "seq", split_axis=0, concat_axis=1, tiled=True),
        lax.all_to_all(dq_rot, "seq", split_axis=0, concat_axis=1, tiled=True),
    )
    dk_copies, dv_copies = (
        lax.all_to_all(
            dk_rot.astype(jnp.bfloat16), "seq", split_axis=0, concat_axis=1, tiled=True
        ).astype(dk_rot.dtype),
        lax.all_to_all(
            dv_all.astype(jnp.bfloat16), "seq", split_axis=0, concat_axis=1, tiled=True
        ).astype(dv_all.dtype),
    )
    dk_tokens = jnp.sum(dk_copies.reshape(tokens, KV, copies, HD), axis=2)
    dv_tokens = jnp.sum(dv_copies.reshape(tokens, KV, copies, HD), axis=2)
    grad_query = rotary_back(dq_tokens.astype(jnp.float32), positions)
    grad_key = rotary_back(dk_tokens, positions)
    sums_query, sums_key, sums_value = lax.psum(
        (
            jnp.sum(grad_query, axis=0).reshape(HQ * HD),
            jnp.sum(grad_key, axis=0).reshape(KV * HD),
            jnp.sum(dv_tokens, axis=0).reshape(KV * HD),
        ),
        ("dp", "seq"),
    )
    return (
        out_tokens.reshape(1, tokens, HQ * HD),
        grad_query.astype(jnp.bfloat16).reshape(1, tokens, HQ * HD),
        grad_key.astype(jnp.bfloat16).reshape(1, tokens, KV * HD),
        dv_tokens.astype(jnp.bfloat16).reshape(1, tokens, KV * HD),
        sums_query,
        sums_key,
        sums_value,
    )


def solution(mesh):
    placed = (
        P("dp", "seq", None),
        P("dp", "seq", None),
        P("dp", "seq", None),
        P("dp", "seq", None),
        P("dp", "seq", None),
        P(),
        P(),
        P(),
        P("dp"),
        P("dp", "seq", None),
    )
    return jax.shard_map(
        body,
        mesh=mesh,
        in_specs=placed,
        out_specs=(
            P("dp", "seq", None),
            P("dp", "seq", None),
            P("dp", "seq", None),
            P("dp", "seq", None),
            P(),
            P(),
            P(),
        ),
        check_vma=False,
    )
```

profile of v0, /device:TPU:1, one launch (start us, length us, event | category | flops | bytes accessed | tf_op | source)
XLA Modules:
  0.0 376.5 jit_solution(17324488417311112449)
XLA Ops:
  2.4 6.5 %all-to-all-start.2 = ((bf16[128,8,128]{2,0,1:T(8,128)(2,1)}), bf16[128,8,128]{2,0,1:T(8,128)(2,1)S(1)}, u32[]{:S(2)}, u32[]{:S(2)}) async-start(bf16[128,8,128]{2,0,1:T(8,128)(2,1)} %bitcast.11), calls=%async_computation.2 | async-start | bytes 524288 | tf_op jit(solution)/shard_map/all_to_all | solution.py:158
  15.8 3.4 all-to-all-start.4
  19.3 6.0 %all-to-all-done.4 = bf16[128,8,128]{2,0,1:T(8,128)(2,1)S(1)} async-done(((bf16[128,8,128]{2,0,1:T(8,128)(2,1)}), bf16[128,8,128]{2,0,1:T(8,128)(2,1)S(1)}, u32[]{:S(2)}, u32[]{:S(2)}) %all-to-all-start.4) | async-done | bytes 262176 | tf_op jit(solution)/shard_map/all_to_all | solution.py:159
  26.1 3.4 all-to-all-start.5
  29.8 5.8 %all-to-all-done.5 = bf16[128,8,128]{2,0,1:T(8,128)(2,1)S(1)} async-done(((bf16[128,8,128]{2,0,1:T(8,128)(2,1)}), bf16[128,8,128]{2,0,1:T(8,128)(2,1)S(1)}, u32[]{:S(2)}, u32[]{:S(2)}) %all-to-all-start.5) | async-done | bytes 262176 | tf_op jit(solution)/shard_map/all_to_all | solution.py:154
  36.4 3.4 all-to-all-start.3
  41.2 4.7 %all-to-all-done.3 = bf16[128,8,128]{2,0,1:T(8,128)(2,1)S(1)} async-done(((bf16[128,8,128]{2,0,1:T(8,128)(2,1)}), bf16[128,8,128]{2,0,1:T(8,128)(2,1)S(1)}, u32[]{:S(2)}, u32[]{:S(2)}) %all-to-all-start.3) | async-done | bytes 262176 | tf_op jit(solution)/shard_map/all_to_all | solution.py:153
  45.9 3.7 all-to-all-start.1
  53.5 6.5 %all-to-all-done.1 = bf16[128,32,128]{0,2,1:T(8,128)(2,1)S(1)} async-done(((bf16[128,32,128]{0,2,1:T(8,128)(2,1)}), bf16[128,32,128]{0,2,1:T(8,128)(2,1)S(1)}, u32[]{:S(2)}, u32[]{:S(2)}) %all-to-all-start.1) | async-done | bytes 1048608 | tf_op jit(solution)/shard_map/all_to_all | solution.py:155
  60.0 3.6 all-to-all-start
  66.7 7.2 %all-to-all-done = bf16[128,32,128]{2,0,1:T(8,128)(2,1)S(1)} async-done(((bf16[128,32,128]{2,0,1:T(8,128)(2,1)}), bf16[128,32,128]{2,0,1:T(8,128)(2,1)S(1)}, u32[]{:S(2)}, u32[]{:S(2)}) %all-to-all-start) | async-done | bytes 1048608 | tf_op jit(solution)/shard_map/all_to_all | solution.py:152
  75.0 139.6 %while.59 = (s32[]{:T(128)}, f32[1024,1,128]{2,0,1:T(8,128)S(1)}, f32[1024,1,128]{2,0,1:T(8,128)S(1)}, bf16[4,1024,1,128]{3,1,2,0:T(8,128)(2,1)}, bf16[4,1024,1,...) while((s32[]{:T(128)}, f32[1024,1,128]{2,0,1:T(8,128)S(1)}, ...), condition=%wide.region_6.7_spmd.clone.clone, body=%wide.region_0.6_spmd.clone.clone.sunk | while | flops 1359287296 | bytes 49224388 | solution.py:116
  79.6 28.5 %while.60 = (s32[]{:T(128)}, f32[1024,128]{1,0:T(8,128)S(1)}, f32[1024,128]{1,0:T(8,128)S(1)}, bf16[2,512,1,128]{3,1,0,2:T(8,128)(2,1)}, bf16[2,512,1,128]{3,1,2...) while((s32[]{:T(128)}, f32[1024,128]{1,0:T(8,128)S(1)}, ...), condition=%wide.region_5.5_spmd.clone.clone, body=%wide.region_1.4_spmd.clone.clone.sunk | while | flops 1359025152 | bytes 41875732 | solution.py:104
  114.5 28.5 %while.60 = (s32[]{:T(128)}, f32[1024,128]{1,0:T(8,128)S(1)}, f32[1024,128]{1,0:T(8,128)S(1)}, bf16[2,512,1,128]{3,1,0,2:T(8,128)(2,1)}, bf16[2,512,1,128]{3,1,2...) while((s32[]{:T(128)}, f32[1024,128]{1,0:T(8,128)S(1)}, ...), condition=%wide.region_5.5_spmd.clone.clone, body=%wide.region_1.4_spmd.clone.clone.sunk | while | flops 1359025152 | bytes 41875732 | solution.py:104
  149.4 28.5 %while.60 = (s32[]{:T(128)}, f32[1024,128]{1,0:T(8,128)S(1)}, f32[1024,128]{1,0:T(8,128)S(1)}, bf16[2,512,1,128]{3,1,0,2:T(8,128)(2,1)}, bf16[2,512,1,128]{3,1,2...) while((s32[]{:T(128)}, f32[1024,128]{1,0:T(8,128)S(1)}, ...), condition=%wide.region_5.5_spmd.clone.clone, body=%wide.region_1.4_spmd.clone.clone.sunk | while | flops 1359025152 | bytes 41875732 | solution.py:104
  184.3 28.5 %while.60 = (s32[]{:T(128)}, f32[1024,128]{1,0:T(8,128)S(1)}, f32[1024,128]{1,0:T(8,128)S(1)}, bf16[2,512,1,128]{3,1,0,2:T(8,128)(2,1)}, bf16[2,512,1,128]{3,1,2...) while((s32[]{:T(128)}, f32[1024,128]{1,0:T(8,128)S(1)}, ...), condition=%wide.region_5.5_spmd.clone.clone, body=%wide.region_1.4_spmd.clone.clone.sunk | while | flops 1359025152 | bytes 41875732 | solution.py:104
  216.8 3.4 all-to-all-start.8
  221.8 4.5 %all-to-all-done.8 = bf16[8,2,8192]{2,1,0:T(2,128)(2,1)S(1)} async-done(((bf16[8,2,8192]{2,1,0:T(2,128)(2,1)}), bf16[8,2,8192]{2,1,0:T(2,128)(2,1)S(1)}, u32[]{:S(2)}, u32[]{:S(2)}) %all-to-all-start.8) | async-done | bytes 262176 | tf_op jit(solution)/shard_map/all_to_all | solution.py:172
  226.3 3.6 all-to-all-start.9
  233.0 3.2 all-to-all-done.9
  236.2 3.6 all-to-all-start.6
  241.6 9.9 %all-to-all-done.6 = bf16[1024,4,128]{2,1,0:T(4,128)(2,1)S(1)} async-done(((bf16[1024,4,128]{2,1,0:T(4,128)(2,1)}), bf16[1024,4,128]{2,1,0:T(4,128)(2,1)S(1)}, u32[]{:S(2)}, u32[]{:S(2)}) %all-to-all-start.6) | async-done | bytes 1048608 | tf_op jit(solution)/shard_map/all_to_all | solution.py:168
  251.5 3.6 all-to-all-start.7
  286.0 90.5 %all-reduce = (f32[4096]{0:T(1024)}, f32[512]{0:T(512)}, f32[512]{0:T(512)}) all-reduce(f32[4096]{0:T(1024)S(1)} %bitcast.274, f32[512]{0:T(512)S(1)} %bitcast.276, f32[512]{0:T(512)S(1)} %bitcast.277), channel_id=1, replica_groups=mesh['dp'=32,'seq'=8] {'dp','seq'}, use_global_device_ids=true, to_apply=%region_10.11 | all-reduce | flops 5120 | bytes 40960 | tf_op jit(solution)/shard_map/psum | solution.py:183
  (330 shorter events, 184.0 us)
Async XLA Ops:
  0.6 10.7 %copy-start.22 = (bf16[1,128,512]{2,1,0:T(8,128)(2,1)S(1)}, bf16[1,128,512]{2,1,0:T(8,128)(2,1)}, u32[]{:S(2)}) copy-start(bf16[1,128,512]{2,1,0:T(8,128)(2,1)} %param.15) | copy-start | bytes 393220
  0.6 10.9 %copy-start.23 = (bf16[1,128,512]{2,1,0:T(8,128)(2,1)S(1)}, bf16[1,128,512]{2,1,0:T(8,128)(2,1)}, u32[]{:S(2)}) copy-start(bf16[1,128,512]{2,1,0:T(8,128)(2,1)} %param.18) | copy-start | bytes 393220
  2.4 16.9 %copy-start.25 = (bf16[512]{0:T(512)(128)(2,1)S(1)}, bf16[512]{0:T(512)(128)(2,1)}, u32[]{:S(2)}) copy-start(bf16[512]{0:T(512)(128)(2,1)} %param.20) | copy-start | bytes 3076
  2.4 12.7 %all-to-all-start.2 = ((bf16[128,8,128]{2,0,1:T(8,128)(2,1)}), bf16[128,8,128]{2,0,1:T(8,128)(2,1)S(1)}, u32[]{:S(2)}, u32[]{:S(2)}) async-start(bf16[128,8,128]{2,0,1:T(8,128)(2,1)} %bitcast.11), calls=%async_computation.2 | async-start | bytes 524288 | tf_op jit(solution)/shard_map/all_to_all | solution.py:158
  12.1 37.5 %copy-start.8 = (f32[128,128]{1,0:T(8,128)}, f32[128,128]{1,0:T(8,128)S(1)}, u32[]{:S(2)}) copy-start(f32[128,128]{1,0:T(8,128)S(1)} %get-tuple-element.735) | copy-start | bytes 196612
  12.1 37.6 %copy-start.6 = (f32[128,128]{1,0:T(8,128)}, f32[128,128]{1,0:T(8,128)S(1)}, u32[]{:S(2)}) copy-start(f32[128,128]{1,0:T(8,128)S(1)} %get-tuple-element.734) | copy-start | bytes 196612
  15.8 9.5 %all-to-all-start.4 = ((bf16[128,8,128]{2,0,1:T(8,128)(2,1)}), bf16[128,8,128]{2,0,1:T(8,128)(2,1)S(1)}, u32[]{:S(2)}, u32[]{:S(2)}) async-start(bf16[128,8,128]{2,0,1:T(8,128)(2,1)} %bitcast.21), calls=%async_computation.4 | async-start | bytes 524288 | tf_op jit(solution)/shard_map/all_to_all | solution.py:159
  19.3 20.5 %copy-start.10 = (bf16[1,128,4096]{2,1,0:T(8,128)(2,1)S(1)}, bf16[1,128,4096]{2,1,0:T(8,128)(2,1)}, u32[]{:S(2)}) copy-start(bf16[1,128,4096]{2,1,0:T(8,128)(2,1)} %param.23) | copy-start | bytes 3145732
  25.3 15.8 %copy-start.13 = (bf16[128,8,128]{2,0,1:T(8,128)(2,1)}, bf16[128,8,128]{2,0,1:T(8,128)(2,1)S(1)}, u32[]{:S(2)}) copy-start(bf16[128,8,128]{2,0,1:T(8,128)(2,1)S(1)} %all-to-all-done.4) | copy-start | bytes 786436
  26.1 9.5 %all-to-all-start.5 = ((bf16[128,8,128]{2,0,1:T(8,128)(2,1)}), bf16[128,8,128]{2,0,1:T(8,128)(2,1)S(1)}, u32[]{:S(2)}, u32[]{:S(2)}) async-start(bf16[128,8,128]{2,0,1:T(8,128)(2,1)} %bitcast.26), calls=%async_computation.5 | async-start | bytes 524288 | tf_op jit(solution)/shard_map/all_to_all | solution.py:154
  36.4 9.5 %all-to-all-start.3 = ((bf16[128,8,128]{2,0,1:T(8,128)(2,1)}), bf16[128,8,128]{2,0,1:T(8,128)(2,1)S(1)}, u32[]{:S(2)}, u32[]{:S(2)}) async-start(bf16[128,8,128]{2,0,1:T(8,128)(2,1)} %bitcast.17), calls=%async_computation.3 | async-start | bytes 524288 | tf_op jit(solution)/shard_map/all_to_all | solution.py:153
  39.8 10.0 %copy-start.11 = (bf16[1,128,4096]{2,1,0:T(8,128)(2,1)S(1)}, bf16[1,128,4096]{2,1,0:T(8,128)(2,1)}, u32[]{:S(2)}) copy-start(bf16[1,128,4096]{2,1,0:T(8,128)(2,1)} %param.14) | copy-start | bytes 3145732
  45.9 3.8 %copy-start.17 = (bf16[128,8,128]{2,0,1:T(8,128)(2,1)}, bf16[128,8,128]{2,0,1:T(8,128)(2,1)S(1)}, u32[]{:S(2)}) copy-start(bf16[128,8,128]{2,0,1:T(8,128)(2,1)S(1)} %all-to-all-done.3) | copy-start | bytes 786436
  45.9 4.6 %copy-start.24 = (bf16[4096]{0:T(1024)(128)(2,1)S(1)}, bf16[4096]{0:T(1024)(128)(2,1)}, u32[]{:S(2)}) copy-start(bf16[4096]{0:T(1024)(128)(2,1)} %param.19) | copy-start | bytes 24580
  45.9 14.1 %all-to-all-start.1 = ((bf16[128,32,128]{0,2,1:T(8,128)(2,1)}), bf16[128,32,128]{0,2,1:T(8,128)(2,1)S(1)}, u32[]{:S(2)}, u32[]{:S(2)}) async-start(bf16[128,32,128]{0,2,1:T(8,128)(2,1)} %bitcast.6), calls=%async_computation.1 | async-start | bytes 2097152 | tf_op jit(solution)/shard_map/all_to_all | solution.py:155
  52.2 11.4 %copy-start.14 = (bf16[128,8,128]{2,0,1:T(8,128)(2,1)S(1)}, bf16[128,8,128]{2,0,1:T(8,128)(2,1)}, u32[]{:S(2)}) copy-start(bf16[128,8,128]{2,0,1:T(8,128)(2,1)} %copy-done.13) | copy-start | bytes 786436
  52.2 11.4 %copy-start.16 = (bf16[128,8,128]{2,0,1:T(8,128)(2,1)S(1)}, bf16[128,8,128]{2,0,1:T(8,128)(2,1)}, u32[]{:S(2)}) copy-start(bf16[128,8,128]{2,0,1:T(8,128)(2,1)} %copy-done.15) | copy-start | bytes 786436
  60.0 13.9 %all-to-all-start = ((bf16[128,32,128]{2,0,1:T(8,128)(2,1)}), bf16[128,32,128]{2,0,1:T(8,128)(2,1)S(1)}, u32[]{:S(2)}, u32[]{:S(2)}) async-start(bf16[128,32,128]{2,0,1:T(8,128)(2,1)} %copy.142), calls=%async_computation | async-start | bytes 2097152 | tf_op jit(solution)/shard_map/all_to_all | solution.py:152
  216.8 9.5 %all-to-all-start.8 = ((bf16[8,2,8192]{2,1,0:T(2,128)(2,1)}), bf16[8,2,8192]{2,1,0:T(2,128)(2,1)S(1)}, u32[]{:S(2)}, u32[]{:S(2)}) async-start(bf16[8,2,8192]{2,1,0:T(2,128)(2,1)} %reshape.436), calls=%async_computation.8 | async-start | bytes 524288 | tf_op jit(solution)/shard_map/all_to_all | solution.py:172
  226.3 10.0 %all-to-all-start.9 = ((bf16[8,2,8192]{2,1,0:T(2,128)(2,1)}), bf16[8,2,8192]{2,1,0:T(2,128)(2,1)S(1)}, u32[]{:S(2)}, u32[]{:S(2)}) async-start(bf16[8,2,8192]{2,1,0:T(2,128)(2,1)} %reshape.438), calls=%async_computation.9 | async-start | bytes 524288 | tf_op jit(solution)/shard_map/all_to_all | solution.py:175
  229.9 9.9 %copy-start.12 = (bf16[4,1024,1,128]{3,1,2,0:T(8,128)(2,1)S(1)}, bf16[4,1024,1,128]{3,1,2,0:T(8,128)(2,1)}, u32[]{:S(2)}) copy-start(bf16[4,1024,1,128]{3,1,2,0:T(8,128)(2,1)} %get-tuple-element.348) | copy-start | bytes 3145732
  236.2 15.3 %all-to-all-start.6 = ((bf16[1024,4,128]{2,1,0:T(4,128)(2,1)}), bf16[1024,4,128]{2,1,0:T(4,128)(2,1)S(1)}, u32[]{:S(2)}, u32[]{:S(2)}) async-start(bf16[1024,4,128]{2,1,0:T(4,128)(2,1)} %copy.153), calls=%async_computation.6 | async-start | bytes 2097152 | tf_op jit(solution)/shard_map/all_to_all | solution.py:168
  251.5 16.6 %all-to-all-start.7 = ((bf16[1024,4,128]{2,1,0:T(4,128)(2,1)}), bf16[1024,4,128]{2,1,0:T(4,128)(2,1)S(1)}, u32[]{:S(2)}, u32[]{:S(2)}) async-start(bf16[1024,4,128]{2,1,0:T(4,128)(2,1)} %bitcast.260), calls=%async_computation.7 | async-start | bytes 2097152 | tf_op jit(solution)/shard_map/all_to_all | solution.py:169
  255.4 5.0 %copy-start.9 = (f32[128,128]{1,0:T(8,128)S(1)}, f32[128,128]{1,0:T(8,128)}, u32[]{:S(2)}) copy-start(f32[128,128]{1,0:T(8,128)} %copy-done.8) | copy-start | bytes 196612
  (25 other events, 60.5 us)
where the time goes:
time: 379 us; the launch traced here: 376 us
  blocking collectives  90.5 us (24%)
  matrix products  79 us (21%)
  local copies, waits for them, and re-layouts  62 us (16%)
  waiting for transfers between devices  53.1 us (14%)
  starting transfers between devices  38.1 us (10%)
  other arithmetic  37.6 us (10%)
  loops' own time  14.1 us (4%)
    psum x1, blocking collectives, body(): lax.psum((jnp.sum(grad_query, axis=0).reshape(HQ * HD), jnp.sum(grad_key,...  90.5 us
    dot_general x8, matrix products, row_step(): jnp.einsum('hrk,kd->rhd', dscore, key_one, preferred_element_type=jnp.flo...  24.6 us
    dot_general x8, matrix products, row_step(): jnp.einsum('rhd,kd->hrk', cot_rows, value_one, preferred_element_type=jnp...  19.4 us
    dot_general x8, matrix products, row_step(): jnp.einsum('rhd,kd->hrk', query_rows, key_one, preferred_element_type=jnp...  18.6 us
    all_to_all x1, waiting for transfers between devices, body(): lax.all_to_all(outputs, 'seq', split_axis=0, concat_axis=1, tiled=True)  9.94 us
    another operation x1, loops' own time, attend(): lax.scan(head_step, (zeros_kv, zeros_kv), jnp.arange(heads // head_block,...  8.13 us
    unnamed x57, local copies, waits for them, and re-layouts  7.6 us
  transfers between devices with their start and end apart: 10, of which 10 were waited for; matrix products, arithmetic and copies ran while one was open for 7% of the time, Pallas kernels for 0%

commit v1 on v0

--- a/solution.py
+++ b/solution.py
@@ -1,3 +1,4 @@
+import functools
 import jax
 import jax.numpy as jnp
 from jax import lax
@@ -7,6 +8,22 @@
 KV = 4
 HD = 128
 GROUP = 8
+
+
+def hold_terms(tile_in, lane_axis, in_dim, axis_k):
+    x_next = jnp.concatenate(
+        lax.all_to_all(
+            jnp.stack(jnp.split(tile_in, lax.axis_size(lane_axis), in_dim), 0),
+            axis_name=lane_axis,
+            split_axis=0,
+            concat_axis=0,
+        ),
+        axis_k,
+    )
+    return x_next
+
+
+detail_stocks = functools.partial(hold_terms, lane_axis="seq", in_dim=1, axis_k=0)
 
 
 def rotary_tables(positions, width):
@@ -152,7 +169,7 @@
         lax.all_to_all(queries, "seq", split_axis=1, concat_axis=0, tiled=True),
         lax.all_to_all(keys_wide, "seq", split_axis=1, concat_axis=0, tiled=True),
         lax.all_to_all(values_wide, "seq", split_axis=1, concat_axis=0, tiled=True),
-        lax.all_to_all(cotangent, "seq", split_axis=1, concat_axis=0, tiled=True),
+        detail_stocks(cotangent),
     )
     head_cache_keys, head_cache_values = (
         lax.all_to_all(cache_keys_wide, "seq", split_axis=1, concat_axis=0, tiled=True),

time: 379 us -> 390 us (1.029)
  local copies, waits for them, and re-layouts: 62 us -> 73 us
  waiting for transfers between devices: 53.1 us -> 48.7 us
    split x0 -> x9, local copies, waits for them, and re-layouts: none -> 7.15 us  [hold_terms(): jnp.split(tile_in, lax.axis_size(lane_axis), in_dim)]
    unnamed x57 -> x76, local copies, waits for them, and re-layouts: 7.6 us -> 8.68 us
  transfers between devices with their start and end apart: 10 -> 10, of which waited for: 10 -> 9; matrix products, arithmetic and copies ran while one was open for 7% -> 10% of each run, Pallas kernels for 0% -> 0%
where the time goes in v1:
time: 390 us; the launch traced here: 388 us
  blocking collectives  90.7 us (23%)
  matrix products  79.2 us (20%)
  local copies, waits for them, and re-layouts  73 us (19%)
  waiting for transfers between devices  48.7 us (12%)
  starting transfers between devices  41.3 us (11%)
  other arithmetic  38.4 us (10%)
  loops' own time  14.2 us (4%)
    psum x1, blocking collectives, body(): lax.psum((jnp.sum(grad_query, axis=0).reshape(HQ * HD), jnp.sum(grad_key,...  90.7 us
    dot_general x8, matrix products, row_step(): jnp.einsum('hrk,kd->rhd', dscore, key_one, preferred_element_type=jnp.flo...  24.7 us
    dot_general x8, matrix products, row_step(): jnp.einsum('rhd,kd->hrk', cot_rows, value_one, preferred_element_type=jnp...  19.5 us
    dot_general x8, matrix products, row_step(): jnp.einsum('rhd,kd->hrk', query_rows, key_one, preferred_element_type=jnp...  18.5 us
    all_to_all x1, waiting for transfers between devices, body(): lax.all_to_all(queries, 'seq', split_axis=1, concat_axis=0, tiled=True)  9.26 us
    all_to_all x1, waiting for transfers between devices, body(): lax.all_to_all(outputs, 'seq', split_axis=0, concat_axis=1, tiled=True)  9.24 us
    unnamed x76, local copies, waits for them, and re-layouts  8.68 us
    another operation x1, loops' own time, attend(): lax.scan(head_step, (zeros_kv, zeros_kv), jnp.arange(heads // head_block,...  8.2 us
  transfers between devices with their start and end apart: 10, of which 9 were waited for; matrix products, arithmetic and copies ran while one was open for 10% of the time, Pallas kernels for 0%

profile of v1, /device:TPU:1, one launch (start us, length us, event | category | flops | bytes accessed | tf_op | source)
XLA Modules:
  0.0 387.5 jit_solution(6441683339130237077)
XLA Ops:
  2.4 6.4 %all-to-all-start.2 = ((bf16[128,8,128]{2,0,1:T(8,128)(2,1)}), bf16[128,8,128]{2,0,1:T(8,128)(2,1)}, u32[]{:S(2)}, u32[]{:S(2)}) async-start(bf16[128,8,128]{2,0,1:T(8,128)(2,1)} %bitcast.16), calls=%async_computation.2 | async-start | bytes 524288 | tf_op jit(solution)/shard_map/all_to_all | solution.py:175
  23.2 5.1 %all-to-all-start.4 = ((bf16[128,8,128]{2,0,1:T(8,128)(2,1)}), bf16[128,8,128]{2,0,1:T(8,128)(2,1)S(1)}, u32[]{:S(2)}, u32[]{:S(2)}) async-start(bf16[128,8,128]{2,0,1:T(8,128)(2,1)} %bitcast.26), calls=%async_computation.4 | async-start | bytes 524288 | tf_op jit(solution)/shard_map/all_to_all | solution.py:176
  29.3 5.2 %all-to-all-done.4 = bf16[128,8,128]{2,0,1:T(8,128)(2,1)S(1)} async-done(((bf16[128,8,128]{2,0,1:T(8,128)(2,1)}), bf16[128,8,128]{2,0,1:T(8,128)(2,1)S(1)}, u32[]{:S(2)}, u32[]{:S(2)}) %all-to-all-start.4) | async-done | bytes 262176 | tf_op jit(solution)/shard_map/all_to_all | solution.py:176
  35.3 4.1 %all-to-all-start.5 = ((bf16[128,8,128]{2,0,1:T(8,128)(2,1)}), bf16[128,8,128]{2,0,1:T(8,128)(2,1)}, u32[]{:S(2)}, u32[]{:S(2)}) async-start(bf16[128,8,128]{2,0,1:T(8,128)(2,1)} %bitcast.31), calls=%async_computation.5 | async-start | bytes 524288 | tf_op jit(solution)/shard_map/all_to_all | solution.py:171
  40.0 5.5 %all-to-all-done.5 = bf16[128,8,128]{2,0,1:T(8,128)(2,1)} async-done(((bf16[128,8,128]{2,0,1:T(8,128)(2,1)}), bf16[128,8,128]{2,0,1:T(8,128)(2,1)}, u32[]{:S(2)}, u32[]{:S(2)}) %all-to-all-start.5) | async-done | bytes 262176 | tf_op jit(solution)/shard_map/all_to_all | solution.py:171
  47.1 4.0 %all-to-all-start.3 = ((bf16[128,8,128]{2,0,1:T(8,128)(2,1)}), bf16[128,8,128]{2,0,1:T(8,128)(2,1)}, u32[]{:S(2)}, u32[]{:S(2)}) async-start(bf16[128,8,128]{2,0,1:T(8,128)(2,1)} %bitcast.22), calls=%async_computation.3 | async-start | bytes 524288 | tf_op jit(solution)/shard_map/all_to_all | solution.py:170
  54.2 3.2 all-to-all-done.3
  57.3 3.6 all-to-all-start
  62.2 9.3 %all-to-all-done = bf16[128,32,128]{2,0,1:T(8,128)(2,1)S(1)} async-done(((bf16[128,32,128]{2,0,1:T(8,128)(2,1)}), bf16[128,32,128]{2,0,1:T(8,128)(2,1)S(1)}, u32[]{:S(2)}, u32[]{:S(2)}) %all-to-all-start) | async-done | bytes 1048608 | tf_op jit(solution)/shard_map/all_to_all | solution.py:169
  71.4 4.0 %all-to-all-start.1 = ((bf16[8,128,4,128]{3,1,2,0:T(8,128)(2,1)}), bf16[8,128,4,128]{3,1,2,0:T(8,128)(2,1)S(1)}, u32[]{:S(2)}, u32[]{:S(2)}) async-start(bf16[8,128,4,128]{3,1,2,0:T(8,128)(2,1)} %copy-done.8), calls=%async_computation.1 | async-start | bytes 2097152 | tf_op jit(solution)/shard_map/all_to_all | solution.py:15
  78.5 7.2 %all-to-all-done.1 = bf16[8,128,4,128]{3,1,2,0:T(8,128)(2,1)S(1)} async-done(((bf16[8,128,4,128]{3,1,2,0:T(8,128)(2,1)}), bf16[8,128,4,128]{3,1,2,0:T(8,128)(2,1)S(1)}, u32[]{:S(2)}, u32[]{:S(2)}) %all-to-all-start.1) | async-done | bytes 1048608 | tf_op jit(solution)/shard_map/all_to_all | solution.py:15
  86.9 140.3 %while.59 = (s32[]{:T(128)}, f32[1024,1,128]{2,0,1:T(8,128)S(1)}, f32[1024,1,128]{2,0,1:T(8,128)S(1)}, bf16[4,1024,1,128]{3,1,2,0:T(8,128)(2,1)}, bf16[4,1024,1,...) while((s32[]{:T(128)}, f32[1024,1,128]{2,0,1:T(8,128)S(1)}, ...), condition=%wide.region_6.7_spmd.clone.clone, body=%wide.region_0.6_spmd.clone.clone.sunk | while | flops 1359287296 | bytes 53418744 | solution.py:133
  91.6 28.6 %while.60 = (s32[]{:T(128)}, f32[1024,128]{1,0:T(8,128)S(1)}, f32[1024,128]{1,0:T(8,128)S(1)}, bf16[2,512,1,128]{3,1,0,2:T(8,128)(2,1)}, bf16[2,512,1,128]{3,1,2...) while((s32[]{:T(128)}, f32[1024,128]{1,0:T(8,128)S(1)}, ...), condition=%wide.region_5.5_spmd.clone.clone, body=%wide.region_1.4_spmd.clone.clone.sunk | while | flops 1359025152 | bytes 41875732 | solution.py:121
  126.6 28.6 %while.60 = (s32[]{:T(128)}, f32[1024,128]{1,0:T(8,128)S(1)}, f32[1024,128]{1,0:T(8,128)S(1)}, bf16[2,512,1,128]{3,1,0,2:T(8,128)(2,1)}, bf16[2,512,1,128]{3,1,2...) while((s32[]{:T(128)}, f32[1024,128]{1,0:T(8,128)S(1)}, ...), condition=%wide.region_5.5_spmd.clone.clone, body=%wide.region_1.4_spmd.clone.clone.sunk | while | flops 1359025152 | bytes 41875732 | solution.py:121
  161.7 28.6 %while.60 = (s32[]{:T(128)}, f32[1024,128]{1,0:T(8,128)S(1)}, f32[1024,128]{1,0:T(8,128)S(1)}, bf16[2,512,1,128]{3,1,0,2:T(8,128)(2,1)}, bf16[2,512,1,128]{3,1,2...) while((s32[]{:T(128)}, f32[1024,128]{1,0:T(8,128)S(1)}, ...), condition=%wide.region_5.5_spmd.clone.clone, body=%wide.region_1.4_spmd.clone.clone.sunk | while | flops 1359025152 | bytes 41875732 | solution.py:121
  196.8 28.6 %while.60 = (s32[]{:T(128)}, f32[1024,128]{1,0:T(8,128)S(1)}, f32[1024,128]{1,0:T(8,128)S(1)}, bf16[2,512,1,128]{3,1,0,2:T(8,128)(2,1)}, bf16[2,512,1,128]{3,1,2...) while((s32[]{:T(128)}, f32[1024,128]{1,0:T(8,128)S(1)}, ...), condition=%wide.region_5.5_spmd.clone.clone, body=%wide.region_1.4_spmd.clone.clone.sunk | while | flops 1359025152 | bytes 41875732 | solution.py:121
  229.4 3.4 all-to-all-start.8
  234.4 4.5 %all-to-all-done.8 = bf16[8,2,8192]{2,1,0:T(2,128)(2,1)S(1)} async-done(((bf16[8,2,8192]{2,1,0:T(2,128)(2,1)}), bf16[8,2,8192]{2,1,0:T(2,128)(2,1)S(1)}, u32[]{:S(2)}, u32[]{:S(2)}) %all-to-all-start.8) | async-done | bytes 262176 | tf_op jit(solution)/shard_map/all_to_all | solution.py:189
  238.8 3.4 all-to-all-start.9
  248.3 3.6 all-to-all-start.6
  253.7 9.2 %all-to-all-done.6 = bf16[1024,4,128]{2,1,0:T(4,128)(2,1)S(1)} async-done(((bf16[1024,4,128]{2,1,0:T(4,128)(2,1)}), bf16[1024,4,128]{2,1,0:T(4,128)(2,1)S(1)}, u32[]{:S(2)}, u32[]{:S(2)}) %all-to-all-start.6) | async-done | bytes 1048608 | tf_op jit(solution)/shard_map/all_to_all | solution.py:185
  262.9 3.8 all-to-all-start.7
  283.9 3.2 copy.206
  296.9 90.7 %all-reduce = (f32[4096]{0:T(1024)}, f32[512]{0:T(512)}, f32[512]{0:T(512)}) all-reduce(f32[4096]{0:T(1024)S(1)} %bitcast.286, f32[512]{0:T(512)S(1)} %bitcast.288, f32[512]{0:T(512)S(1)} %bitcast.289), channel_id=1, replica_groups=mesh['dp'=32,'seq'=8] {'dp','seq'}, use_global_device_ids=true, to_apply=%region_10.11 | all-reduce | flops 5120 | bytes 40960 | tf_op jit(solution)/shard_map/psum | solution.py:200
  (375 shorter events, 192.1 us)
Async XLA Ops:
  0.6 11.4 %copy-start.30 = (bf16[1,128,512]{2,1,0:T(8,128)(2,1)S(1)}, bf16[1,128,512]{2,1,0:T(8,128)(2,1)}, u32[]{:S(2)}) copy-start(bf16[1,128,512]{2,1,0:T(8,128)(2,1)} %param.15) | copy-start | bytes 393220
  0.6 11.7 %copy-start.31 = (bf16[1,128,512]{2,1,0:T(8,128)(2,1)S(1)}, bf16[1,128,512]{2,1,0:T(8,128)(2,1)}, u32[]{:S(2)}) copy-start(bf16[1,128,512]{2,1,0:T(8,128)(2,1)} %param.18) | copy-start | bytes 393220
  0.7 12.4 %copy-start.29 = (bf16[1,128,512]{2,1,0:T(8,128)(2,1)S(1)}, bf16[1,128,512]{2,1,0:T(8,128)(2,1)}, u32[]{:S(2)}) copy-start(bf16[1,128,512]{2,1,0:T(8,128)(2,1)} %param.16) | copy-start | bytes 393220
  1.7 12.2 %copy-start.11 = (bf16[1,128,4096]{2,1,0:T(8,128)(2,1)S(1)}, bf16[1,128,4096]{2,1,0:T(8,128)(2,1)}, u32[]{:S(2)}) copy-start(bf16[1,128,4096]{2,1,0:T(8,128)(2,1)} %param.14) | copy-start | bytes 3145732
  2.4 20.0 %all-to-all-start.2 = ((bf16[128,8,128]{2,0,1:T(8,128)(2,1)}), bf16[128,8,128]{2,0,1:T(8,128)(2,1)}, u32[]{:S(2)}, u32[]{:S(2)}) async-start(bf16[128,8,128]{2,0,1:T(8,128)(2,1)} %bitcast.16), calls=%async_computation.2 | async-start | bytes 524288 | tf_op jit(solution)/shard_map/all_to_all | solution.py:175
  10.6 17.9 %copy-start.6 = (f32[128,128]{1,0:T(8,128)}, f32[128,128]{1,0:T(8,128)S(1)}, u32[]{:S(2)}) copy-start(f32[128,128]{1,0:T(8,128)S(1)} %get-tuple-element.742) | copy-start | bytes 196612
  10.6 17.9 %copy-start.9 = (f32[128,128]{1,0:T(8,128)}, f32[128,128]{1,0:T(8,128)S(1)}, u32[]{:S(2)}) copy-start(f32[128,128]{1,0:T(8,128)S(1)} %get-tuple-element.743) | copy-start | bytes 196612
  15.2 7.2 %copy-start.19 = (bf16[128,4,128]{2,0,1:T(8,128)(2,1)S(1)}, bf16[128,4,128]{2,0,1:T(8,128)(2,1)}, u32[]{:S(2)}) copy-start(bf16[128,4,128]{2,0,1:T(8,128)(2,1)} %copy.193) | copy-start | bytes 393220
  20.9 13.7 %copy-start.18 = (bf16[128,4,128]{2,0,1:T(8,128)(2,1)S(1)}, bf16[128,4,128]{2,0,1:T(8,128)(2,1)}, u32[]{:S(2)}) copy-start(bf16[128,4,128]{2,0,1:T(8,128)(2,1)} %copy.194) | copy-start | bytes 393220
  22.4 16.9 %copy-start.32 = (bf16[4096]{0:T(1024)(128)(2,1)S(1)}, bf16[4096]{0:T(1024)(128)(2,1)}, u32[]{:S(2)}) copy-start(bf16[4096]{0:T(1024)(128)(2,1)} %param.19) | copy-start | bytes 24580
  23.2 11.3 %all-to-all-start.4 = ((bf16[128,8,128]{2,0,1:T(8,128)(2,1)}), bf16[128,8,128]{2,0,1:T(8,128)(2,1)S(1)}, u32[]{:S(2)}, u32[]{:S(2)}) async-start(bf16[128,8,128]{2,0,1:T(8,128)(2,1)} %bitcast.26), calls=%async_computation.4 | async-start | bytes 524288 | tf_op jit(solution)/shard_map/all_to_all | solution.py:176
  35.3 10.2 %all-to-all-start.5 = ((bf16[128,8,128]{2,0,1:T(8,128)(2,1)}), bf16[128,8,128]{2,0,1:T(8,128)(2,1)}, u32[]{:S(2)}, u32[]{:S(2)}) async-start(bf16[128,8,128]{2,0,1:T(8,128)(2,1)} %bitcast.31), calls=%async_computation.5 | async-start | bytes 524288 | tf_op jit(solution)/shard_map/all_to_all | solution.py:171
  47.1 10.2 %all-to-all-start.3 = ((bf16[128,8,128]{2,0,1:T(8,128)(2,1)}), bf16[128,8,128]{2,0,1:T(8,128)(2,1)}, u32[]{:S(2)}, u32[]{:S(2)}) async-start(bf16[128,8,128]{2,0,1:T(8,128)(2,1)} %bitcast.22), calls=%async_computation.3 | async-start | bytes 524288 | tf_op jit(solution)/shard_map/all_to_all | solution.py:170
  52.8 8.1 %copy-start.28 = (bf16[128,4,128]{2,0,1:T(8,128)(2,1)S(1)}, bf16[128,4,128]{2,0,1:T(8,128)(2,1)}, u32[]{:S(2)}) copy-start(bf16[128,4,128]{2,0,1:T(8,128)(2,1)} %copy.181) | copy-start | bytes 393220
  52.8 8.1 %copy-start.27 = (bf16[128,4,128]{2,0,1:T(8,128)(2,1)S(1)}, bf16[128,4,128]{2,0,1:T(8,128)(2,1)}, u32[]{:S(2)}) copy-start(bf16[128,4,128]{2,0,1:T(8,128)(2,1)} %copy.182) | copy-start | bytes 393220
  52.8 8.1 %copy-start.26 = (bf16[128,4,128]{2,0,1:T(8,128)(2,1)S(1)}, bf16[128,4,128]{2,0,1:T(8,128)(2,1)}, u32[]{:S(2)}) copy-start(bf16[128,4,128]{2,0,1:T(8,128)(2,1)} %copy.183) | copy-start | bytes 393220
  52.8 8.2 %copy-start.25 = (bf16[128,4,128]{2,0,1:T(8,128)(2,1)S(1)}, bf16[128,4,128]{2,0,1:T(8,128)(2,1)}, u32[]{:S(2)}) copy-start(bf16[128,4,128]{2,0,1:T(8,128)(2,1)} %copy.184) | copy-start | bytes 393220
  57.3 14.1 %all-to-all-start = ((bf16[128,32,128]{2,0,1:T(8,128)(2,1)}), bf16[128,32,128]{2,0,1:T(8,128)(2,1)S(1)}, u32[]{:S(2)}, u32[]{:S(2)}) async-start(bf16[128,32,128]{2,0,1:T(8,128)(2,1)} %copy.178), calls=%async_computation | async-start | bytes 2097152 | tf_op jit(solution)/shard_map/all_to_all | solution.py:169
  71.4 14.3 %all-to-all-start.1 = ((bf16[8,128,4,128]{3,1,2,0:T(8,128)(2,1)}), bf16[8,128,4,128]{3,1,2,0:T(8,128)(2,1)S(1)}, u32[]{:S(2)}, u32[]{:S(2)}) async-start(bf16[8,128,4,128]{3,1,2,0:T(8,128)(2,1)} %copy-done.8), calls=%async_computation.1 | async-start | bytes 2097152 | tf_op jit(solution)/shard_map/all_to_all | solution.py:15
  229.4 9.5 %all-to-all-start.8 = ((bf16[8,2,8192]{2,1,0:T(2,128)(2,1)}), bf16[8,2,8192]{2,1,0:T(2,128)(2,1)S(1)}, u32[]{:S(2)}, u32[]{:S(2)}) async-start(bf16[8,2,8192]{2,1,0:T(2,128)(2,1)} %reshape.440), calls=%async_computation.8 | async-start | bytes 524288 | tf_op jit(solution)/shard_map/all_to_all | solution.py:189
  238.8 9.5 %all-to-all-start.9 = ((bf16[8,2,8192]{2,1,0:T(2,128)(2,1)}), bf16[8,2,8192]{2,1,0:T(2,128)(2,1)S(1)}, u32[]{:S(2)}, u32[]{:S(2)}) async-start(bf16[8,2,8192]{2,1,0:T(2,128)(2,1)} %reshape.442), calls=%async_computation.9 | async-start | bytes 524288 | tf_op jit(solution)/shard_map/all_to_all | solution.py:192
  242.3 9.6 %copy-start.13 = (bf16[4,1024,1,128]{3,1,2,0:T(8,128)(2,1)S(1)}, bf16[4,1024,1,128]{3,1,2,0:T(8,128)(2,1)}, u32[]{:S(2)}) copy-start(bf16[4,1024,1,128]{3,1,2,0:T(8,128)(2,1)} %get-tuple-element.348) | copy-start | bytes 3145732
  248.3 14.6 %all-to-all-start.6 = ((bf16[1024,4,128]{2,1,0:T(4,128)(2,1)}), bf16[1024,4,128]{2,1,0:T(4,128)(2,1)S(1)}, u32[]{:S(2)}, u32[]{:S(2)}) async-start(bf16[1024,4,128]{2,1,0:T(4,128)(2,1)} %copy.196), calls=%async_computation.6 | async-start | bytes 2097152 | tf_op jit(solution)/shard_map/all_to_all | solution.py:185
  262.9 16.0 %all-to-all-start.7 = ((bf16[1024,4,128]{2,1,0:T(4,128)(2,1)}), bf16[1024,4,128]{2,1,0:T(4,128)(2,1)S(1)}, u32[]{:S(2)}, u32[]{:S(2)}) async-start(bf16[1024,4,128]{2,1,0:T(4,128)(2,1)} %bitcast.273), calls=%async_computation.7 | async-start | bytes 2097152 | tf_op jit(solution)/shard_map/all_to_all | solution.py:186
  (39 other events, 112.4 us)
